TPU v7x, 128 devices: a whole 4x4x4 slice. The times are simulated.
128 devices in a mesh: region: 16 (over y_lo, z, core), group: 8 (over y_hi, x).
Axes of the slice: x: 4, y: 4 (y_hi: 2, y_lo: 2; y = y_hi * 2 + y_lo), z: 4, core: 2. Of those that a mesh axis runs over, the one named last changes fastest.
Arguments:
- object_slab: float32 [8192, 2, 4096], P('region', None, 'group'), may hold values from -6 to 6
- probe: float32 [4, 2, 256, 256], replicated, may hold values from -6 to 6
- diffraction: float32 [512, 256, 256], P(('region', 'group')), may hold values from 0.25 to 16
- positions: int32 [512, 2], P(('region', 'group')), may hold values from 0 to 7936, as said below
- slot_counts: int32 [8, 16], P('group', 'region'), may hold values from 1 to 4, 40 in all within a row
Outputs:
- new_object: float32 [8192, 2, 4096], P('region', None, 'group')
- new_probe: float32 [4, 2, 256, 256], replicated
Inputs may be any that keep to these rules, and one draw needn't show every extreme that they name: `positions`: A slot of region index r has its row in r * 512 to min(r * 512 + 511, 7936); columns lie in 0 to 256; rows 0 and 7936 and columns 0 and 256 are each taken by some slot.
All inputs are finite; a program needn't handle non-finite values. No bound on the sum of `slot_counts` on one device may be relied on, other than what follows from the above.
Results may differ from a plain program's by a relative error of at most 0.0003.
Values sent between devices are 32-bit elements; how exact they have to be, the bound alone decides.
A program may use at most 128 MiB of HBM per device.

v0:
```python
import math
import jax
import jax.numpy as jnp
from jax import lax
from jax.sharding import PartitionSpec as P

highest = lax.Precision.HIGHEST


def shifted(block, axis, distance):
    devices = range(lax.axis_size(axis))
    route = [(i - distance, i) for i in devices if i - distance in devices]
    return lax.ppermute(block, axis, route)


def tables(side):
    index = jnp.arange(side, dtype=jnp.int32)
    prod = index[:, None] * index[None, :] % side
    angle = prod.astype(jnp.float32) * (2.0 * math.pi / side)
    scale = 1.0 / math.sqrt(side)
    return (jnp.cos(angle) * scale, -jnp.sin(angle) * scale)


def transform(real_part, imag_part, cos_tab, sin_tab):
    left_r = jnp.einsum("jk,mkl->mjl", cos_tab, real_part, precision=highest) - jnp.einsum(
        "jk,mkl->mjl", sin_tab, imag_part, precision=highest
    )
    left_i = jnp.einsum("jk,mkl->mjl", cos_tab, imag_part, precision=highest) + jnp.einsum(
        "jk,mkl->mjl", sin_tab, real_part, precision=highest
    )
    out_r = jnp.einsum("mjk,kl->mjl", left_r, cos_tab, precision=highest) - jnp.einsum(
        "mjk,kl->mjl", left_i, sin_tab, precision=highest
    )
    out_i = jnp.einsum("mjk,kl->mjl", left_r, sin_tab, precision=highest) + jnp.einsum(
        "mjk,kl->mjl", left_i, cos_tab, precision=highest
    )
    return (out_r, out_i)


def on_device(object_slab, probe, diffraction, positions, slot_counts):
    side = probe.shape[2]
    slots = diffraction.shape[0]
    tile_rows = object_slab.shape[0]
    active_count = slot_counts[0, 0]
    cos_tab, sin_tab = tables(side)
    base = lax.axis_index("region") * tile_rows
    local_rows = positions[:, 0] - base
    shard_columns = positions[:, 1]
    obj = object_slab
    prb = probe
    peak = jnp.max(jnp.sum(prb[:, 0] * prb[:, 0] + prb[:, 1] * prb[:, 1], axis=0))
    below = shifted(obj, "region", -1)
    extended = jnp.concatenate([obj, below], axis=0)

    def cut(row, col):
        return lax.dynamic_slice(extended, (row, jnp.int32(0), col), (side, 2, side))

    windows = jax.vmap(cut)(local_rows, shard_columns)
    probe_r = prb[:, 0]
    probe_i = prb[:, 1]

    def single_position(position_entry, carry):
        wgrads, pgrad, cover = carry
        live = (position_entry < active_count).astype(jnp.float32)
        win = lax.dynamic_index_in_dim(windows, position_entry, 0, keepdims=False)
        observed_intensity = lax.dynamic_index_in_dim(
            diffraction, position_entry, 0, keepdims=False
        )
        win_r = win[:, 0, :]
        win_i = win[:, 1, :]
        exit_r = probe_r * win_r[None] - probe_i * win_i[None]
        exit_i = probe_r * win_i[None] + probe_i * win_r[None]
        far_r, far_i = transform(exit_r, exit_i, cos_tab, sin_tab)
        model_intensity = jnp.sum(far_r * far_r + far_i * far_i, axis=0)
        update_ratio = 1.0 - jnp.sqrt(observed_intensity) / jnp.sqrt(
            jnp.maximum(model_intensity, 1.0)
        )
        chi_r, chi_i = transform(
            far_r * update_ratio[None], far_i * update_ratio[None], cos_tab, -sin_tab
        )
        chi_r = chi_r * live
        chi_i = chi_i * live
        go_r = jnp.sum(probe_r * chi_r + probe_i * chi_i, axis=0)
        go_i = jnp.sum(probe_r * chi_i - probe_i * chi_r, axis=0)
        grad_win = jnp.stack([go_r, go_i], axis=1)
        wgrads = lax.dynamic_update_index_in_dim(wgrads, grad_win, position_entry, 0)
        gp = jnp.stack(
            [win_r[None] * chi_r + win_i[None] * chi_i, win_r[None] * chi_i - win_i[None] * chi_r],
            axis=1,
        )
        return (wgrads, pgrad + gp, cover + live * (win_r * win_r + win_i * win_i))

    start_carry = (
        jnp.zeros((slots, side, 2, side), jnp.float32),
        jnp.zeros(prb.shape, jnp.float32),
        jnp.zeros((side, side), jnp.float32),
    )
    wgrads, pgrad, cover = lax.fori_loop(0, slots, single_position, start_carry)
    pgrad, cover = lax.psum((pgrad, cover), ("region", "group"))

    def put(position_entry, scratch_array):
        row = local_rows[position_entry]
        col = shard_columns[position_entry]
        current = lax.dynamic_slice(scratch_array, (row, jnp.int32(0), col), (side, 2, side))
        return lax.dynamic_update_slice(
            scratch_array, current + wgrads[position_entry], (row, jnp.int32(0), col)
        )

    scratch_array = lax.fori_loop(0, slots, put, jnp.zeros(extended.shape, jnp.float32))
    tile_grad = scratch_array[:tile_rows]
    spill = scratch_array[tile_rows:]
    arrived = shifted(spill, "region", 1)
    tile_grad = tile_grad + arrived
    obj = obj - tile_grad / peak
    prb = prb - pgrad / (cover + 1e-06)[None, None]
    return (obj, prb)


def solution(mesh):
    placed = (
        P("region", None, "group"),
        P(),
        P(("region", "group"), None, None),
        P(("region", "group"), None),
        P("group", "region"),
    )
    return jax.shard_map(
        on_device,
        mesh=mesh,
        in_specs=placed,
        out_specs=(P("region", None, "group"), P()),
        check_vma=False,
    )
```

profile of v0, /device:TPU:1, one launch (start us, length us, event | category | flops | bytes accessed | tf_op | source)
XLA Modules:
  0.0 704.6 jit_solution(1375702932699397892)
XLA Ops:
  7.2 3.3 collective-permute-start
  13.6 22.5 %collective-permute-done = f32[512,2,512]{2,1,0:T(2,128)} collective-permute-done((f32[512,2,512]{2,1,0:T(2,128)}, f32[512,2,512]{2,1,0:T(2,128)}, u32[]{:S(2)}, u32[]{:S(2)}) %collective-permute-start) | collective-permute-done | bytes 2097184 | tf_op jit(solution)/shard_map/ppermute | solution.py:13
  36.2 5.3 pad_maximum_fusion
  43.4 17.1 %while.35 = (s32[]{:T(128)}, f32[1024,2,512]{2,1,0:T(2,128)}, s32[4,3]{1,0:T(4,128)S(1)}, f32[4,256,2,256]{3,2,1,0:T(2,128)}, s32[]{:T(128)}) while((s32[]{:T(128)}, f32[1024,2,512]{2,1,0:T(2,128)}, s32[4,3]{1,0:T(4,128)S(1)}, f32[4,256,2,256]{3,2,1,0:T(2,128)}, s32[]{:T(128)}) %tuple.99), condition=%wide.while_cond, body=%wide.while_body.sunk | while | flops 2 | bytes 1050217 | solution.py:56
  43.9 3.7 bitcast_dynamic-update-slice_fusion.2
  48.2 3.7 bitcast_dynamic-update-slice_fusion.2
  52.5 3.7 bitcast_dynamic-update-slice_fusion.2
  56.8 3.7 bitcast_dynamic-update-slice_fusion.2
  62.3 249.9 %while.36 = (s32[]{:T(128)}, f32[4,256,2,256]{3,2,1,0:T(2,128)}, f32[4,2,256,256]{3,2,0,1:T(8,128)}, f32[256,256]{1,0:T(8,128)}, f32[4,256,2,256]{3,2,1,0:T(2,12...) while((s32[]{:T(128)}, f32[4,256,2,256]{3,2,1,0:T(2,128)}, ...), condition=%wide.region_4.5_spmd.clone.clone, body=%wide.region_0.4_spmd.clone.clone.sunk | while | flops 12915048448 | bytes 82838280 | solution.py:98
  63.9 2.7 fusion.223
  66.7 2.7 fusion.224
  69.4 2.7 fusion.220
  72.1 2.7 fusion.221
  74.9 3.2 fusion.222
  87.2 2.8 fusion.230
  90.0 3.7 fusion.231
  100.1 3.7 fusion.229
  104.4 4.6 fusion.232
  111.7 5.4 add_bitcast_fusion.2
  117.0 3.2 maximum_add_fusion.2
  124.3 2.7 fusion.223
  127.1 2.7 fusion.224
  129.8 2.7 fusion.220
  132.5 2.7 fusion.221
  135.3 2.8 fusion.222
  143.5 2.7 add_reduce_fusion.4
  147.2 2.9 fusion.230
  150.1 3.7 fusion.231
  160.1 3.7 fusion.229
  164.5 4.8 fusion.232
  172.0 5.4 add_bitcast_fusion.2
  177.3 3.9 maximum_add_fusion.2
  186.0 2.7 fusion.223
  188.7 2.7 fusion.224
  191.5 2.7 fusion.220
  194.2 2.7 fusion.221
  197.0 2.9 fusion.222
  208.9 3.1 fusion.230
  212.0 3.7 fusion.231
  222.1 3.7 fusion.229
  226.4 4.5 fusion.232
  233.6 5.4 add_bitcast_fusion.2
  239.0 3.9 maximum_add_fusion.2
  247.7 2.7 fusion.223
  250.5 2.7 fusion.224
  253.2 2.7 fusion.220
  255.9 2.7 fusion.221
  258.7 3.1 fusion.222
  270.8 2.8 fusion.230
  273.7 3.7 fusion.231
  283.7 3.7 fusion.229
  288.1 4.6 fusion.232
  295.3 5.4 add_bitcast_fusion.2
  300.7 3.9 maximum_add_fusion.2
  312.3 3.0 broadcast_in_dim.30
  315.3 207.1 %while.34 = (s32[]{:T(128)}, f32[1024,2,512]{2,1,0:T(2,128)}, s32[4]{0:T(128)S(1)}, s32[4]{0:T(128)S(1)}, f32[4,256,2,256]{3,2,1,0:T(2,128)}, /*index=5*/s32[]{:T(128)}, s32[]{:T(128)}, s32[]{:T(128)}, s32[]{:T(128)}) while((s32[]{:T(128)}, f32[1024,2,512]{2,1,0:T(2,128)}, s32[4]{0:T(128)S(1)}, s32[4]{0:T(128)S(1)}, ...), condition=%wide.region_6.7_spmd, body=%wide.region_5.6_spmd.sunk | while | flops 131080 | bytes 2621641 | solution.py:109
  322.1 45.0 %dynamic_update_slice.21 = f32[1024,2,512]{2,1,0:T(2,128)} dynamic-update-slice(f32[1024,2,512]{2,1,0:T(2,128)} %get-tuple-element.735, f32[256,2,256]{2,1,0:T(2,128)S(1)} %bitcast_add_fusion.2, s32[]{:T(128)S(6)} %select_n.175, s32[]{:T(128)} %constant.116.clone.1..sunk, s32[]{:T(128)S(6)} %select_n.176) | dynamic-update-slice | bytes 1048580 | tf_op jit(solution)/shard_map/while/body/eval_jaxpr/dynamic_update_slice | solution.py:105
  373.8 45.0 %dynamic_update_slice.21 = f32[1024,2,512]{2,1,0:T(2,128)} dynamic-update-slice(f32[1024,2,512]{2,1,0:T(2,128)} %get-tuple-element.735, f32[256,2,256]{2,1,0:T(2,128)S(1)} %bitcast_add_fusion.2, s32[]{:T(128)S(6)} %select_n.175, s32[]{:T(128)} %constant.116.clone.1..sunk, s32[]{:T(128)S(6)} %select_n.176) | dynamic-update-slice | bytes 1048580 | tf_op jit(solution)/shard_map/while/body/eval_jaxpr/dynamic_update_slice | solution.py:105
  425.6 45.0 %dynamic_update_slice.21 = f32[1024,2,512]{2,1,0:T(2,128)} dynamic-update-slice(f32[1024,2,512]{2,1,0:T(2,128)} %get-tuple-element.735, f32[256,2,256]{2,1,0:T(2,128)S(1)} %bitcast_add_fusion.2, s32[]{:T(128)S(6)} %select_n.175, s32[]{:T(128)} %constant.116.clone.1..sunk, s32[]{:T(128)S(6)} %select_n.176) | dynamic-update-slice | bytes 1048580 | tf_op jit(solution)/shard_map/while/body/eval_jaxpr/dynamic_update_slice | solution.py:105
  477.4 45.0 %dynamic_update_slice.21 = f32[1024,2,512]{2,1,0:T(2,128)} dynamic-update-slice(f32[1024,2,512]{2,1,0:T(2,128)} %get-tuple-element.735, f32[256,2,256]{2,1,0:T(2,128)S(1)} %bitcast_add_fusion.2, s32[]{:T(128)S(6)} %select_n.175, s32[]{:T(128)} %constant.116.clone.1..sunk, s32[]{:T(128)S(6)} %select_n.176) | dynamic-update-slice | bytes 1048580 | tf_op jit(solution)/shard_map/while/body/eval_jaxpr/dynamic_update_slice | solution.py:105
  522.3 3.8 slice.43
  532.0 155.4 %all-reduce.3.cloned.1.call-done = (f32[4,2,256,256]{3,2,1,0:T(8,128)}, f32[256,256]{1,0:T(8,128)}) async-done(((f32[4,2,256,256]{3,2,1,0:T(8,128)}, f32[256,256]{1,0:T(8,128)}), (f32[4,2,256,256]{3,2,1,0:T(8,128)}, f32[256,256]{1,0:T(8,128)})) %all-reduce.3.cloned.1.call-update) | async-done | bytes 2359312 | tf_op jit(solution)/shard_map/psum | solution.py:99
  688.5 3.4 divide_subtract_fusion.1
  692.7 4.9 divide_subtract_fusion
  (137 shorter events, 116.7 us)
Async XLA Ops:
  7.2 680.3 %all-reduce.3.cloned.1.call-start = ((), (), s32[]{:S(2)}) async-start(), calls=%async_computation | async-start | bytes 4718592 | tf_op jit(solution)/shard_map/psum | solution.py:99
  7.2 29.0 %collective-permute-start = (f32[512,2,512]{2,1,0:T(2,128)}, f32[512,2,512]{2,1,0:T(2,128)}, u32[]{:S(2)}, u32[]{:S(2)}) collective-permute-start(f32[512,2,512]{2,1,0:T(2,128)} %param.9), channel_id=1, source_target_pairs={{8,0},{16,8},{24,16},{32,24},{40,32},{48,40},{56,48},{64,56},{72,6... | collective-permute-start | bytes 6291464 | tf_op jit(solution)/shard_map/ppermute | solution.py:13
  11.7 24.5 %copy-start.7 = (f32[512,2,512]{2,1,0:T(2,128)S(1)}, f32[512,2,512]{2,1,0:T(2,128)}, u32[]{:S(2)}) copy-start(f32[512,2,512]{2,1,0:T(2,128)} %param.9) | copy-start | bytes 6291460
  99.0 1.0 copy-start.1
  104.4 4.6 copy-start.2
  104.4 7.3 %copy-start = (f32[4,256,256]{1,2,0:T(8,128)S(1)}, f32[4,256,256]{1,2,0:T(8,128)}, u32[]{:S(2)}) copy-start(f32[4,256,256]{1,2,0:T(8,128)} %fusion.231) | copy-start | bytes 3145732 | tf_op jit(solution)/shard_map/while
  117.0 3.2 copy-start.5
  159.1 1.0 copy-start.1
  164.5 4.8 copy-start.2
  164.5 7.5 %copy-start = (f32[4,256,256]{1,2,0:T(8,128)S(1)}, f32[4,256,256]{1,2,0:T(8,128)}, u32[]{:S(2)}) copy-start(f32[4,256,256]{1,2,0:T(8,128)} %fusion.231) | copy-start | bytes 3145732 | tf_op jit(solution)/shard_map/while
  177.3 3.9 copy-start.5
  221.0 1.0 copy-start.1
  226.4 4.6 copy-start.2
  226.4 7.2 %copy-start = (f32[4,256,256]{1,2,0:T(8,128)S(1)}, f32[4,256,256]{1,2,0:T(8,128)}, u32[]{:S(2)}) copy-start(f32[4,256,256]{1,2,0:T(8,128)} %fusion.231) | copy-start | bytes 3145732 | tf_op jit(solution)/shard_map/while
  239.0 3.9 copy-start.5
  282.7 1.0 copy-start.1
  288.0 4.6 copy-start.2
  288.1 7.3 %copy-start = (f32[4,256,256]{1,2,0:T(8,128)S(1)}, f32[4,256,256]{1,2,0:T(8,128)}, u32[]{:S(2)}) copy-start(f32[4,256,256]{1,2,0:T(8,128)} %fusion.231) | copy-start | bytes 3145732 | tf_op jit(solution)/shard_map/while
  300.7 3.9 copy-start.5
  522.3 5.7 copy-start.3
  526.2 165.7 %collective-permute-start.1 = (f32[512,2,512]{2,1,0:T(2,128)}, f32[512,2,512]{2,1,0:T(2,128)}, u32[]{:S(2)}, u32[]{:S(2)}) collective-permute-start(f32[512,2,512]{2,1,0:T(2,128)} %slice.43), channel_id=1, source_target_pairs={{0,8},{8,16},{16,24},{24,32},{32,40},{40,48},{48,56},{56,64},{64,7... | collective-permute-start | bytes 6291464 | tf_op jit(solution)/shard_map/ppermute | solution.py:13
  529.6 1.6 copy-start.6
  688.4 3.4 copy-start.4
  688.4 4.2 copy-start.8
Sparse Core Ops, SparseCore 0:
  529.8 157.6 all-reduce.2
where the time goes:
time: 710 us; the launch traced here: 705 us
  local copies, waits for them, and re-layouts  230 us (32%)
  matrix products  201 us (28%)
  waiting for transfers between devices  178 us (25%)
  other arithmetic  53.2 us (7%)
  loops' own time  23.3 us (3%)
  between operations  14.3 us (2%)
    dynamic_update_slice x4, local copies, waits for them, and re-layouts, put(): lax.dynamic_update_slice(scratch_array, current + wgrads[position_entry],...  180 us
    psum x1, waiting for transfers between devices, on_device(): pgrad, cover = lax.psum((pgrad, cover), ('region', 'group'))  155 us
    dot_general x8, matrix products, transform(): jnp.einsum('mjk,kl->mjl', left_i, sin_tab, precision=highest)  32.1 us
    dot_general x8, matrix products, transform(): jnp.einsum('mjk,kl->mjl', left_i, cos_tab, precision=highest)  29.2 us
    dot_general x8, matrix products, transform(): jnp.einsum('jk,mkl->mjl', sin_tab, real_part, precision=highest)  25.5 us
    dot_general x8, matrix products, transform(): jnp.einsum('mjk,kl->mjl', left_r, sin_tab, precision=highest)  25.3 us
    dot_general x8, matrix products, transform(): jnp.einsum('mjk,kl->mjl', left_r, cos_tab, precision=highest)  22.6 us
    ppermute x2, waiting for transfers between devices, shifted(): return lax.ppermute(block, axis, route)  22.5 us
  transfers between devices with their start and end apart: 3, of which 2 were waited for; matrix products, arithmetic and copies ran while one was open for 1% of the time, Pallas kernels for 0%

commit v1 on v0

--- a/solution.py
+++ b/solution.py
@@ -96,7 +96,13 @@
         jnp.zeros((side, side), jnp.float32),
     )
     wgrads, pgrad, cover = lax.fori_loop(0, slots, single_position, start_carry)
-    pgrad, cover = lax.psum((pgrad, cover), ("region", "group"))
+
+    def state_push(inputs):
+        for at in ("region", "group"):
+            inputs = lax.psum(inputs, at)
+        return inputs
+
+    pgrad, cover = state_push((pgrad, cover))
 
     def put(position_entry, scratch_array):
         row = local_rows[position_entry]

time: 710 us -> 649 us (0.914)
  waiting for transfers between devices: 178 us -> 111 us
    psum x1 -> x2, waiting for transfers between devices: 155 us -> 65.9 us  [state_push(): inputs = lax.psum(inputs, at)]
    ppermute x2, waiting for transfers between devices: 22.5 us -> 44.9 us  [shifted(): return lax.ppermute(block, axis, route)]
  transfers between devices with their start and end apart: 3 -> 4, of which waited for: 2 -> 3; matrix products, arithmetic and copies ran while one was open for 1% -> 33% of each run, Pallas kernels for 0% -> 0%
where the time goes in v1:
time: 649 us; the launch traced here: 639 us
  local copies, waits for them, and re-layouts  230 us (35%)
  matrix products  200 us (31%)
  waiting for transfers between devices  111 us (17%)
  other arithmetic  53.3 us (8%)
  loops' own time  25 us (4%)
  between operations  14.3 us (2%)
    dynamic_update_slice x4, local copies, waits for them, and re-layouts, put(): lax.dynamic_update_slice(scratch_array, current + wgrads[position_entry],...  180 us
    psum x2, waiting for transfers between devices, state_push(): inputs = lax.psum(inputs, at)  65.9 us
    ppermute x2, waiting for transfers between devices, shifted(): return lax.ppermute(block, axis, route)  44.9 us
    dot_general x8, matrix products, transform(): jnp.einsum('mjk,kl->mjl', left_i, sin_tab, precision=highest)  32.1 us
    dot_general x8, matrix products, transform(): jnp.einsum('mjk,kl->mjl', left_i, cos_tab, precision=highest)  29.2 us
    dot_general x8, matrix products, transform(): jnp.einsum('jk,mkl->mjl', sin_tab, real_part, precision=highest)  25.5 us
    dot_general x8, matrix products, transform(): jnp.einsum('mjk,kl->mjl', left_r, sin_tab, precision=highest)  25.3 us
    dot_general x8, matrix products, transform(): jnp.einsum('mjk,kl->mjl', left_r, cos_tab, precision=highest)  22.6 us
  transfers between devices with their start and end apart: 4, of which 3 were waited for; matrix products, arithmetic and copies ran while one was open for 33% of the time, Pallas kernels for 0%

profile of v1, /device:TPU:1, one launch (start us, length us, event | category | flops | bytes accessed | tf_op | source)
XLA Modules:
  0.0 639.3 jit_solution(3221936872275931441)
XLA Ops:
  7.2 3.3 collective-permute-start
  13.6 22.5 %collective-permute-done = f32[512,2,512]{2,1,0:T(2,128)} collective-permute-done((f32[512,2,512]{2,1,0:T(2,128)}, f32[512,2,512]{2,1,0:T(2,128)}, u32[]{:S(2)}, u32[]{:S(2)}) %collective-permute-start) | collective-permute-done | bytes 2097184 | tf_op jit(solution)/shard_map/ppermute | solution.py:13
  36.2 5.3 pad_maximum_fusion
  43.4 17.9 %while.35 = (s32[]{:T(128)}, f32[1024,2,512]{2,1,0:T(2,128)}, s32[4,3]{1,0:T(4,128)S(1)}, f32[4,256,2,256]{3,2,1,0:T(2,128)}, s32[]{:T(128)}) while((s32[]{:T(128)}, f32[1024,2,512]{2,1,0:T(2,128)}, s32[4,3]{1,0:T(4,128)S(1)}, f32[4,256,2,256]{3,2,1,0:T(2,128)}, s32[]{:T(128)}) %tuple.99), condition=%wide.while_cond, body=%wide.while_body.sunk | while | flops 2 | bytes 1050217 | solution.py:56
  44.0 3.8 bitcast_dynamic-update-slice_fusion.2
  48.5 3.8 bitcast_dynamic-update-slice_fusion.2
  53.0 3.8 bitcast_dynamic-update-slice_fusion.2
  57.4 3.8 bitcast_dynamic-update-slice_fusion.2
  63.1 249.8 %while.36 = (s32[]{:T(128)}, f32[4,256,2,256]{3,2,1,0:T(2,128)}, f32[4,2,256,256]{3,2,0,1:T(8,128)}, f32[256,256]{1,0:T(8,128)}, f32[4,256,2,256]{3,2,1,0:T(2,12...) while((s32[]{:T(128)}, f32[4,256,2,256]{3,2,1,0:T(2,128)}, ...), condition=%wide.region_4.5_spmd.clone.clone, body=%wide.region_0.4_spmd.clone.clone.sunk | while | flops 12915048448 | bytes 82838280 | solution.py:98
  67.4 2.7 fusion.224
  70.2 2.7 fusion.220
  72.9 2.7 fusion.221
  75.6 3.2 fusion.222
  87.9 2.8 fusion.230
  90.8 3.6 fusion.231
  100.8 3.7 fusion.229
  105.1 4.6 fusion.232
  112.4 5.3 add_bitcast_fusion.2
  117.8 3.2 maximum_add_fusion.2
  125.0 2.7 fusion.223
  127.8 2.7 fusion.224
  130.5 2.7 fusion.220
  133.3 2.7 fusion.221
  136.0 2.8 fusion.222
  147.9 2.9 fusion.230
  150.8 3.6 fusion.231
  160.8 3.7 fusion.229
  165.2 4.8 fusion.232
  172.7 5.3 add_bitcast_fusion.2
  178.0 3.9 maximum_add_fusion.2
  186.7 2.7 fusion.223
  189.4 2.7 fusion.224
  192.2 2.7 fusion.220
  194.9 2.7 fusion.221
  197.6 2.9 fusion.222
  209.6 3.1 fusion.230
  212.7 3.6 fusion.231
  222.7 3.7 fusion.229
  227.1 4.5 fusion.232
  234.3 5.3 add_bitcast_fusion.2
  239.6 3.9 maximum_add_fusion.2
  248.4 2.7 fusion.223
  251.1 2.7 fusion.224
  253.9 2.7 fusion.220
  256.6 2.7 fusion.221
  259.3 3.1 fusion.222
  271.5 2.8 fusion.230
  274.4 3.6 fusion.231
  284.4 3.7 fusion.229
  288.7 4.6 fusion.232
  296.0 5.3 add_bitcast_fusion.2
  301.3 3.9 maximum_add_fusion.2
  312.9 3.1 copy.72
  316.1 3.0 broadcast_in_dim.30
  319.1 209.0 %while.34 = (s32[]{:T(128)}, f32[1024,2,512]{2,1,0:T(2,128)}, s32[4]{0:T(128)S(1)}, s32[4]{0:T(128)S(1)}, f32[4,256,2,256]{3,2,1,0:T(2,128)}, /*index=5*/s32[]{:T(128)}, s32[]{:T(128)}, s32[]{:T(128)}, s32[]{:T(128)}) while((s32[]{:T(128)}, f32[1024,2,512]{2,1,0:T(2,128)}, s32[4]{0:T(128)S(1)}, s32[4]{0:T(128)S(1)}, ...), condition=%wide.region_6.7_spmd, body=%wide.region_5.6_spmd.sunk | while | flops 131080 | bytes 2621641 | solution.py:115
  326.4 45.0 %dynamic_update_slice.21 = f32[1024,2,512]{2,1,0:T(2,128)} dynamic-update-slice(f32[1024,2,512]{2,1,0:T(2,128)} %get-tuple-element.737, f32[256,2,256]{2,1,0:T(2,128)S(1)} %bitcast_add_fusion.2, s32[]{:T(128)S(6)} %select_n.175, s32[]{:T(128)} %constant.116.clone.1..sunk, s32[]{:T(128)S(6)} %select_n.176) | dynamic-update-slice | bytes 1048580 | tf_op jit(solution)/shard_map/while/body/eval_jaxpr/dynamic_update_slice | solution.py:111
  378.6 45.0 %dynamic_update_slice.21 = f32[1024,2,512]{2,1,0:T(2,128)} dynamic-update-slice(f32[1024,2,512]{2,1,0:T(2,128)} %get-tuple-element.737, f32[256,2,256]{2,1,0:T(2,128)S(1)} %bitcast_add_fusion.2, s32[]{:T(128)S(6)} %select_n.175, s32[]{:T(128)} %constant.116.clone.1..sunk, s32[]{:T(128)S(6)} %select_n.176) | dynamic-update-slice | bytes 1048580 | tf_op jit(solution)/shard_map/while/body/eval_jaxpr/dynamic_update_slice | solution.py:111
  430.9 45.0 %dynamic_update_slice.21 = f32[1024,2,512]{2,1,0:T(2,128)} dynamic-update-slice(f32[1024,2,512]{2,1,0:T(2,128)} %get-tuple-element.737, f32[256,2,256]{2,1,0:T(2,128)S(1)} %bitcast_add_fusion.2, s32[]{:T(128)S(6)} %select_n.175, s32[]{:T(128)} %constant.116.clone.1..sunk, s32[]{:T(128)S(6)} %select_n.176) | dynamic-update-slice | bytes 1048580 | tf_op jit(solution)/shard_map/while/body/eval_jaxpr/dynamic_update_slice | solution.py:111
  483.1 45.0 %dynamic_update_slice.21 = f32[1024,2,512]{2,1,0:T(2,128)} dynamic-update-slice(f32[1024,2,512]{2,1,0:T(2,128)} %get-tuple-element.737, f32[256,2,256]{2,1,0:T(2,128)S(1)} %bitcast_add_fusion.2, s32[]{:T(128)S(6)} %select_n.175, s32[]{:T(128)} %constant.116.clone.1..sunk, s32[]{:T(128)S(6)} %select_n.176) | dynamic-update-slice | bytes 1048580 | tf_op jit(solution)/shard_map/while/body/eval_jaxpr/dynamic_update_slice | solution.py:111
  528.1 3.6 slice.43
  534.7 22.4 %collective-permute-done.1 = f32[512,2,512]{2,1,0:T(2,128)} collective-permute-done((f32[512,2,512]{2,1,0:T(2,128)}, f32[512,2,512]{2,1,0:T(2,128)}, u32[]{:S(2)}, u32[]{:S(2)}) %collective-permute-start.1) | collective-permute-done | bytes 2097184 | tf_op jit(solution)/shard_map/ppermute | solution.py:13
  557.1 5.2 divide_subtract_fusion
  562.2 65.8 %all-reduce.7.cloned.1.call-done = (f32[4,2,256,256]{3,2,1,0:T(8,128)}, f32[256,256]{1,0:T(8,128)}) async-done(((f32[4,2,256,256]{3,2,1,0:T(8,128)}, f32[256,256]{1,0:T(8,128)}), (f32[4,2,256,256]{3,2,1,0:T(8,128)}, f32[256,256]{1,0:T(8,128)})) %all-reduce.7.cloned.1.call-update) | async-done | bytes 2359312 | tf_op jit(solution)/shard_map/psum | solution.py:102
  629.1 3.2 divide_subtract_fusion.1
  (134 shorter events, 119.0 us)
Async XLA Ops:
  7.2 526.6 %all-reduce.5.cloned.1.call-start = ((), (), s32[]{:S(2)}) async-start(), calls=%async_computation | async-start | bytes 4718592 | tf_op jit(solution)/shard_map/psum | solution.py:102
  7.2 29.0 %collective-permute-start = (f32[512,2,512]{2,1,0:T(2,128)}, f32[512,2,512]{2,1,0:T(2,128)}, u32[]{:S(2)}, u32[]{:S(2)}) collective-permute-start(f32[512,2,512]{2,1,0:T(2,128)} %param.9), channel_id=1, source_target_pairs={{8,0},{16,8},{24,16},{32,24},{40,32},{48,40},{56,48},{64,56},{72,6... | collective-permute-start | bytes 6291464 | tf_op jit(solution)/shard_map/ppermute | solution.py:13
  11.7 24.5 %copy-start.5 = (f32[512,2,512]{2,1,0:T(2,128)S(1)}, f32[512,2,512]{2,1,0:T(2,128)}, u32[]{:S(2)}) copy-start(f32[512,2,512]{2,1,0:T(2,128)} %param.9) | copy-start | bytes 6291460
  99.8 1.0 copy-start.1
  105.1 4.6 copy-start.2
  105.1 7.3 %copy-start = (f32[4,256,256]{1,2,0:T(8,128)S(1)}, f32[4,256,256]{1,2,0:T(8,128)}, u32[]{:S(2)}) copy-start(f32[4,256,256]{1,2,0:T(8,128)} %fusion.231) | copy-start | bytes 3145732 | tf_op jit(solution)/shard_map/while
  117.8 3.2 copy-start.3
  159.8 1.0 copy-start.1
  165.2 4.8 copy-start.2
  165.2 7.5 %copy-start = (f32[4,256,256]{1,2,0:T(8,128)S(1)}, f32[4,256,256]{1,2,0:T(8,128)}, u32[]{:S(2)}) copy-start(f32[4,256,256]{1,2,0:T(8,128)} %fusion.231) | copy-start | bytes 3145732 | tf_op jit(solution)/shard_map/while
  178.0 3.9 copy-start.3
  221.7 1.0 copy-start.1
  227.0 4.6 copy-start.2
  227.1 7.2 %copy-start = (f32[4,256,256]{1,2,0:T(8,128)S(1)}, f32[4,256,256]{1,2,0:T(8,128)}, u32[]{:S(2)}) copy-start(f32[4,256,256]{1,2,0:T(8,128)} %fusion.231) | copy-start | bytes 3145732 | tf_op jit(solution)/shard_map/while
  239.6 3.9 copy-start.3
  283.4 1.0 copy-start.1
  288.7 4.6 copy-start.2
  288.7 7.3 %copy-start = (f32[4,256,256]{1,2,0:T(8,128)S(1)}, f32[4,256,256]{1,2,0:T(8,128)}, u32[]{:S(2)}) copy-start(f32[4,256,256]{1,2,0:T(8,128)} %fusion.231) | copy-start | bytes 3145732 | tf_op jit(solution)/shard_map/while
  301.3 3.9 copy-start.3
  316.0 312.1 %all-reduce.7.cloned.1.call-start = ((), (), s32[]{:S(2)}) async-start(), calls=%async_computation.1 | async-start | bytes 4718592 | tf_op jit(solution)/shard_map/psum | solution.py:102
  531.7 2.1 copy-start.4
  531.7 25.3 %collective-permute-start.1 = (f32[512,2,512]{2,1,0:T(2,128)}, f32[512,2,512]{2,1,0:T(2,128)}, u32[]{:S(2)}, u32[]{:S(2)}) collective-permute-start(f32[512,2,512]{2,1,0:T(2,128)} %slice.43), channel_id=1, source_target_pairs={{0,8},{8,16},{16,24},{24,32},{32,40},{40,48},{48,56},{56,64},{64,7... | collective-permute-start | bytes 6291464 | tf_op jit(solution)/shard_map/ppermute | solution.py:13
Sparse Core Ops, SparseCore 0:
  316.1 129.3 all-reduce.4
  534.0 94.0 all-reduce.6
